TPU v7x, 32 devices: a whole 2x2x4 slice. The times are simulated.
32 devices in a mesh: mem: 4 (over x, core), lon: 8 (over z, y).
Axes of the slice: x: 2, y: 2, z: 4, core: 2. Of those that a mesh axis runs over, the one named last changes fastest.
Arguments:
- controls: bfloat16 [2048, 32, 1024], P('lon', 'mem'), may hold values from -6 to 6
- perturbations: bfloat16 [2048, 32, 1024], P(None, 'mem', 'lon'), may hold values from -0.59765625 to 0.59765625
- lat_factor: bfloat16 [1024, 1024], P('mem'), may hold values from -0.09375 to 0.09375
- lon_factor: bfloat16 [2048, 2048], P('mem'), may hold values from -0.0625 to 0.0625
- obs_index: int32 [4, 8, 32768], P('mem', 'lon'), may hold values from 0 to 65535
- obs_weight: float32 [4, 8, 32768], P('mem', 'lon'), may hold values from 1 to 30
- obs_count: int32 [4, 8], P('mem', 'lon'), may hold values from 8193 to 32768, as said below
Outputs:
- hessian_product: float32 [2048, 32, 1024], P('lon', 'mem')
Inputs may be any that keep to these rules, and one draw needn't show every extreme that they name: `obs_index`: several slots may name one grid point; grid points are numbered with latitude fastest within a tile of 512 by 128. `obs_count`: slots 0 to count - 1 of a tile are in use; some tile uses all 32768 slots.
All inputs are finite; a program needn't handle non-finite values.
Results may differ from a plain program's by a relative error of at most 0.008.
Values may be sent and summed in bfloat16 or wider, within the bound.
No kernel may reach another device: no remote copies, remote signals or barrier semaphores. Data moves between devices by JAX's collectives and lax.ppermute only.
A program may use at most 128 MiB of HBM per device.

v0:
```python
import jax
import jax.numpy as jnp
from jax import lax
from jax.sharding import PartitionSpec as P


def observe(grid_field, index_rows, weight_rows, count_rows):
    tile_count, slot_count = index_rows.shape
    flattened = grid_field.reshape(-1)
    tile_cells = flattened.shape[0] // tile_count
    where_at = index_rows + (jnp.arange(tile_count, dtype=jnp.int32) * tile_cells)[:, None]
    in_use = jnp.arange(slot_count, dtype=jnp.int32)[None, :] < count_rows[:, None]
    picked = flattened[where_at]
    values = jnp.where(in_use, weight_rows * picked, jnp.zeros_like(picked))
    return (
        jnp.zeros_like(flattened)
        .at[where_at.reshape(-1)]
        .add(values.reshape(-1))
        .reshape(grid_field.shape)
    )


def local(controls, perturbations, lat_factor, lon_factor, obs_index, obs_weight, obs_count):
    lon_dev, mem_dev, lat_all = controls.shape
    lat_full = lax.all_gather(lat_factor, "mem", axis=0, tiled=True)
    control_rows = controls.reshape(lon_dev * mem_dev, lat_all)
    banded = (
        control_rows.astype(jnp.float32)
        + lax.dot_general(
            control_rows, lat_full, (((1,), (1,)), ((), ())), preferred_element_type=jnp.float32
        )
    ).astype(jnp.bfloat16)
    moved = lax.all_to_all(
        banded.reshape(lon_dev, mem_dev, lat_all), "lon", split_axis=2, concat_axis=0, tiled=True
    )
    lon_all, _, lat_band = moved.shape
    columns = moved.reshape(lon_all, mem_dev * lat_band)
    lon_full = lax.all_gather(lon_factor, "mem", axis=0, tiled=True)
    spread_fwd = jnp.dot(lon_full, columns, preferred_element_type=jnp.float32)
    localized = columns.astype(jnp.float32) + spread_fwd
    weighted_fwd = (
        perturbations.reshape(lon_all, mem_dev * lat_band).astype(jnp.float32) * localized
    )
    partial_sum = jnp.sum(weighted_fwd.reshape(lon_all, mem_dev, lat_band), axis=1)
    slot_count = obs_index.shape[-1]
    tile_sum = lax.psum_scatter(partial_sum, "mem", scatter_dimension=0, tiled=True)
    grad_tile = observe(
        tile_sum,
        obs_index.reshape(-1, slot_count),
        obs_weight.reshape(-1, slot_count),
        obs_count.reshape(-1),
    ).astype(jnp.bfloat16)
    gradient = lax.all_gather(grad_tile, "mem", axis=0, tiled=True)
    weighted = (
        (perturbations.astype(jnp.float32) * gradient.astype(jnp.float32)[:, None, :])
        .astype(jnp.bfloat16)
        .reshape(lon_all, mem_dev * lat_band)
    )
    spread_back = lax.dot_general(
        lon_full, weighted, (((0,), (0,)), ((), ())), preferred_element_type=jnp.float32
    )
    spread = (
        (weighted.astype(jnp.float32) + spread_back)
        .astype(jnp.bfloat16)
        .reshape(lon_all, mem_dev, lat_band)
    )
    returned = lax.all_to_all(spread, "lon", split_axis=0, concat_axis=2, tiled=True)
    back_rows = returned.reshape(lon_dev * mem_dev, lat_all)
    result = (
        control_rows.astype(jnp.float32)
        + back_rows.astype(jnp.float32)
        + jnp.dot(back_rows, lat_full, preferred_element_type=jnp.float32)
    )
    return result.reshape(lon_dev, mem_dev, lat_all)


def solution(mesh):
    in_specs = (
        P("lon", "mem", None),
        P(None, "mem", "lon"),
        P("mem", None),
        P("mem", None),
        P("mem", "lon", None),
        P("mem", "lon", None),
        P("mem", "lon"),
    )
    out_specs = P("lon", "mem", None)
    return jax.shard_map(local, mesh=mesh, in_specs=in_specs, out_specs=out_specs, check_vma=False)
```

profile of v0, /device:TPU:0, one launch (start us, length us, event | category | flops | bytes accessed | tf_op | source)
XLA Modules:
  0.0 709.8 jit_solution(16194023989570546402)
XLA Ops:
  6.5 0.0 all-gather.3.cloned.1.call-start
  6.5 0.7 all-gather.3.cloned.1.call-update
  7.3 0.0 all-gather.5.cloned.1.call-start
  7.3 0.7 all-gather.5.cloned.1.call-update
  8.0 26.2 %all-gather.3.cloned.1.call-done = bf16[1024,1024]{1,0:T(8,128)(2,1)} async-done(((bf16[256,1024]{1,0:T(8,128)(2,1)}), bf16[1024,1024]{1,0:T(8,128)(2,1)}) %all-gather.3.cloned.1.call-update) | async-done | bytes 2097168 | tf_op jit(solution)/shard_map/all_gather | solution.py:25
  34.2 10.8 %fusion.5 = bf16[256,8,1024]{2,1,0:T(8,128)(2,1)} fusion(bf16[256,8,1024]{2,1,0:T(8,128)(2,1)} %param.7, bf16[1024,1024]{1,0:T(8,128)(2,1)} %all-gather.3.cloned.1.call-done), kind=kOutput, calls=%fused_computation.12 | convolution fusion | flops 4301258752 | bytes 10485760 | tf_op jit(solution)/shard_map/dot_general | solution.py:29
  45.0 7.5 %copy.30 = bf16[256,8,1024]{0,1,2:T(8,128)(2,1)} copy(bf16[256,8,1024]{2,1,0:T(8,128)(2,1)} %fusion.5) | data formatting | bytes 8388608 | tf_op jit(solution)/shard_map/reshape | solution.py:34
  52.4 5.6 all-to-all-start
  58.0 0.0 copy-start
  58.0 0.2 reduce-scatter.2.cloned.1.call-start
  58.2 7.7 %copy.29 = f32[2048,8,128]{0,2,1:T(8,128)} copy(bf16[2048,8,128]{2,1,0:T(8,128)(2,1)} %param.8) | data formatting | bytes 12582912 | tf_op jit(solution)/shard_map/convert_element_type | solution.py:55
  65.9 0.0 copy-done
  65.9 0.1 compare_select_fusion
  66.1 85.6 %all-to-all-done = bf16[256,8,1024]{0,1,2:T(8,128)(2,1)} async-done(((bf16[256,8,1024]{0,1,2:T(8,128)(2,1)}), bf16[256,8,1024]{0,1,2:T(8,128)(2,1)}, u32[]{:S(2)}, u32[]{:S(2)}) %all-to-all-start) | async-done | bytes 4194336 | tf_op jit(solution)/shard_map/all_to_all | solution.py:33
  151.7 4.6 copy.31
  156.2 3.4 copy.36
  159.6 0.0 all-gather.5.cloned.1.call-done
  159.6 17.6 %fusion.4 = f32[2048,1024]{0,1:T(8,128)} fusion(f32[2048,8,128]{0,2,1:T(8,128)} %copy.29, bf16[2048,1024]{0,1:T(8,128)(2,1)} %bitcast.61, bf16[2048,2048]{1,0:T(8,128)(2,1)} %all-gather.5.cloned.1.call-done), kind=kOutput, calls=%fused_computation.10 | convolution fusion | flops 8596226048 | bytes 29360128 | tf_op jit(solution)/shard_map/dot_general | solution.py:39
  177.2 5.1 reduce_sum.9
  182.4 0.0 reduce-scatter.2.cloned.1.call-update
  182.4 0.1 compare_select_fusion.1
  183.2 22.4 %reduce-scatter.2.cloned.1.call-done = f32[512,128]{0,1:T(8,128)} async-done(((f32[2048,128]{0,1:T(8,128)}), f32[512,128]{0,1:T(8,128)}) %reduce-scatter.2.cloned.1.call-update) | async-done | bytes 262160 | tf_op jit(solution)/shard_map/reduce_scatter | solution.py:46
  205.6 1.1 copy.32
  206.7 0.0 copy-start.1
  206.7 180.5 %gather_fusion = f32[32768]{0:T(1024)S(1)} fusion(f32[65536]{0:T(1024)S(1)} %bitcast.58, s32[32768]{0:T(1024)S(1)} %broadcast_clamp_fusion), kind=kCustom, calls=%fused_computation | custom fusion | bytes 393216 | tf_op jit(solution)/shard_map/gather | solution.py:13
  387.2 0.0 copy-done.1
  387.3 171.1 %scatter_custom_fusion = f32[65536]{0:T(1024)S(1)} fusion(s32[32768]{0:T(1024)S(1)} %bitcast.67, f32[32768]{0:T(1024)S(1)} %multiply_select_fusion, f32[]{:T(128)} %constant.3.clone.1), kind=kCustom, calls=%fused_computation.23 | custom fusion | flops 32768 | bytes 262148 | tf_op jit(solution)/shard_map/scatter-add | solution.py:18
  558.4 6.8 all_gather.11
  565.2 0.1 convert_element_type.48
  565.3 4.0 multiply_convert_fusion
  569.3 6.7 copy.33
  576.0 14.4 %fusion.3 = bf16[2048,1024]{0,1:T(8,128)(2,1)} fusion(bf16[2048,1024]{0,1:T(8,128)(2,1)} %bitcast.62, bf16[2048,2048]{1,0:T(8,128)(2,1)} %all-gather.5.cloned.1.call-done), kind=kOutput, calls=%fused_computation.8 | convolution fusion | flops 8596226048 | bytes 16777216 | tf_op jit(solution)/shard_map/dot_general | solution.py:59
  590.4 6.7 copy.34
  597.1 0.0 copy-start.2
  597.1 0.0 copy-start.3
  597.1 99.4 %all_to_all.30 = bf16[2048,8,128]{2,1,0:T(8,128)(2,1)S(1)} all-to-all(bf16[2048,8,128]{2,1,0:T(8,128)(2,1)} %copy.34), channel_id=1, replica_groups=mesh['mem'=4,'lon'=8] {'lon'}, dimensions={0} | all-to-all | bytes 8388608 | tf_op jit(solution)/shard_map/all_to_all | solution.py:67
  696.6 0.0 copy-done.2
  696.6 0.0 copy-done.3
  696.6 6.7 fusion.2
  (3 shorter events, 0.1 us)
Async XLA Ops:
  6.5 27.7 %all-gather.3.cloned.1.call-start = ((), (), s32[]{:S(2)}) async-start(), calls=%async_computation.3 | async-start | bytes 2621440 | tf_op jit(solution)/shard_map/all_gather | solution.py:25
  7.3 152.4 %all-gather.5.cloned.1.call-start = ((), (), s32[]{:S(2)}) async-start(), calls=%async_computation.4 | async-start | bytes 10485760 | tf_op jit(solution)/shard_map/all_gather | solution.py:38
  52.4 99.2 %all-to-all-start = ((bf16[256,8,1024]{0,1,2:T(8,128)(2,1)}), bf16[256,8,1024]{0,1,2:T(8,128)(2,1)}, u32[]{:S(2)}, u32[]{:S(2)}) async-start(bf16[256,8,1024]{0,1,2:T(8,128)(2,1)} %copy.30), calls=%async_computation | async-start | bytes 8388608 | tf_op jit(solution)/shard_map/all_to_all | solution.py:33
  58.0 7.9 %copy-start = (s32[1,1,32768]{2,1,0:T(1,128)S(1)}, s32[1,1,32768]{2,1,0:T(1,128)}, u32[]{:S(2)}) copy-start(s32[1,1,32768]{2,1,0:T(1,128)} %param.11) | copy-start | bytes 393220
  58.0 147.6 %reduce-scatter.2.cloned.1.call-start = ((), (), s32[]{:S(2)}) async-start(), calls=%async_computation.5 | async-start | bytes 1310720 | tf_op jit(solution)/shard_map/reduce_scatter | solution.py:46
  206.7 180.6 %copy-start.1 = (f32[1,1,32768]{2,1,0:T(1,128)S(1)}, f32[1,1,32768]{2,1,0:T(1,128)}, u32[]{:S(2)}) copy-start(f32[1,1,32768]{2,1,0:T(1,128)} %param.12) | copy-start | bytes 393220
  597.1 99.4 %copy-start.2 = (bf16[256,8,1024]{2,1,0:T(8,128)(2,1)S(1)}, bf16[256,8,1024]{2,1,0:T(8,128)(2,1)}, u32[]{:S(2)}) copy-start(bf16[256,8,1024]{2,1,0:T(8,128)(2,1)} %param.7) | copy-start | bytes 12582916
  597.1 99.4 %copy-start.3 = (bf16[1024,1024]{1,0:T(8,128)(2,1)S(1)}, bf16[1024,1024]{1,0:T(8,128)(2,1)}, u32[]{:S(2)}) copy-start(bf16[1024,1024]{1,0:T(8,128)(2,1)} %all-gather.3.cloned.1.call-done) | copy-start | bytes 6291460
Sparse Core Ops, SparseCore 0:
  8.9 25.2 all-gather.2
  35.8 58.2 all-gather.4
  182.5 23.0 reduce-scatter.1
where the time goes:
time: 711 us; the launch traced here: 710 us
  local copies, waits for them, and re-layouts  218 us (31%)
  other arithmetic  181 us (25%)
  waiting for transfers between devices  136 us (19%)
  blocking collectives  106 us (15%)
  matrix products  49.4 us (7%)
  between operations  13.8 us (2%)
    gather x1, local copies, waits for them, and re-layouts, observe(): picked = flattened[where_at]  181 us
    scatter-add x1, other arithmetic, observe(): return jnp.zeros_like(flattened).at[where_at.reshape(-1)].add(values.resh...  171 us
    all_to_all x1, blocking collectives, local(): lax.all_to_all(spread, 'lon', split_axis=0, concat_axis=2, tiled=True)  99.4 us
    all_to_all x1, waiting for transfers between devices, local(): lax.all_to_all(banded.reshape(lon_dev, mem_dev, lat_all), 'lon', split_ax...  85.6 us
    all_gather x1, waiting for transfers between devices, local(): lat_full = lax.all_gather(lat_factor, 'mem', axis=0, tiled=True)  26.2 us
    reduce_scatter x1, waiting for transfers between devices, local(): lax.psum_scatter(partial_sum, 'mem', scatter_dimension=0, tiled=True)  22.4 us
    dot_general x1, matrix products, local(): spread_fwd = jnp.dot(lon_full, columns, preferred_element_type=jnp.float32)  17.6 us
    dot_general x1, matrix products, local(): lax.dot_general(lon_full, weighted, (((0,), (0,)), ((), ())), preferred_e...  14.4 us
  transfers between devices with their start and end apart: 4, of which 3 were waited for; matrix products, arithmetic and copies ran while one was open for 5% of the time, Pallas kernels for 0%

commit v1 on v0

v1 whole, which is shorter than its diff:
```python
import functools

import jax
import jax.numpy as jnp
from jax import lax
from jax.experimental import pallas as pl
from jax.experimental.pallas import tpu as pltpu
from jax.sharding import PartitionSpec as P


F32, BF16 = jnp.float32, jnp.bfloat16
ANY = pl.BlockSpec(memory_space=pl.ANY)
VMEM = pl.BlockSpec(memory_space=pltpu.VMEM)
FAR, NEAR = (7, 6, 5, 4), (3, 2, 1, 0)


def weight_map_kernel(chunk, band, count_ref, index_ref, weight_ref, out_ref, acc_ref):
    step = pl.program_id(0)
    rows = acc_ref.shape[0]

    @pl.when(step == 0)
    def _():
        acc_ref[...] = jnp.zeros_like(acc_ref)

    slot = step * chunk + lax.broadcasted_iota(jnp.int32, (1, chunk), 1)
    index = index_ref[...]
    weight = jnp.where(slot < count_ref[0], weight_ref[...], 0.0)
    high = weight.astype(BF16).astype(F32)
    low = weight - high
    at_row = lax.broadcasted_iota(jnp.int32, (rows, chunk), 0) == index // band
    at_col = lax.broadcasted_iota(jnp.int32, (band, chunk), 0) == index % band
    picked = jnp.where(at_row, 1.0, 0.0).astype(BF16)
    spread = jnp.concatenate(
        [jnp.where(at_col, high, 0.0).astype(BF16), jnp.where(at_col, low, 0.0).astype(BF16)], axis=0
    )
    acc_ref[...] += lax.dot_general(
        picked, spread, (((1,), (1,)), ((), ())), preferred_element_type=F32
    )

    @pl.when(step == pl.num_programs(0) - 1)
    def _():
        out_ref[...] = acc_ref[:, :band] + acc_ref[:, band:]


def weight_map(obs_index, obs_weight, obs_count, rows, band):
    slots = obs_index.shape[-1]
    chunk = min(slots, 8192)
    return pl.pallas_call(
        functools.partial(weight_map_kernel, chunk, band),
        out_shape=jax.ShapeDtypeStruct((rows, band), F32),
        grid_spec=pltpu.PrefetchScalarGridSpec(
            num_scalar_prefetch=1,
            grid=(slots // chunk,),
            in_specs=[
                pl.BlockSpec((1, chunk), lambda i, c: (0, i)),
                pl.BlockSpec((1, chunk), lambda i, c: (0, i)),
            ],
            out_specs=pl.BlockSpec((rows, band), lambda i, c: (0, 0)),
            scratch_shapes=[pltpu.VMEM((rows, 2 * band), F32)],
        ),
        cost_estimate=pl.CostEstimate(
            flops=4 * rows * band * slots, bytes_accessed=8 * slots, transcendentals=0
        ),
        compiler_params=pltpu.CompilerParams(vmem_limit_bytes=40 << 20),
        name="weight_map",
    )(obs_count.reshape(1), obs_index.reshape(1, slots), obs_weight.reshape(1, slots))


def low_lanes(shape):
    return lax.broadcasted_iota(jnp.int32, shape, 1) < shape[1] // 2


def swap(value):
    return pltpu.roll(value, value.shape[1] // 2, 1)


def pack(first, second, half):
    mask = low_lanes(first.shape)
    if half == 0:
        return jnp.where(mask, first, swap(second))
    return jnp.where(mask, swap(first), second)


def prepare_perturbations_kernel(members, x_ref, low_ref, high_ref, wide_ref):
    wide_ref[...] = x_ref[...].astype(F32)
    rows = low_ref.shape[0]
    lanes = x_ref.shape[1]
    for pair in range(members // 2):
        first = wide_ref[pl.ds(2 * pair, rows, stride=members), :]
        second = wide_ref[pl.ds(2 * pair + 1, rows, stride=members), :]
        where = slice(pair * lanes, (pair + 1) * lanes)
        low_ref[:, where] = pack(first, second, 0).astype(BF16)
        high_ref[:, where] = pack(first, second, 1).astype(BF16)


def prepare_perturbations(perturbations):
    lon_all, members, band = perturbations.shape
    rows = min(lon_all, 256)
    wide = members * band // 2
    return pl.pallas_call(
        functools.partial(prepare_perturbations_kernel, members),
        out_shape=[jax.ShapeDtypeStruct((lon_all, wide), BF16)] * 2,
        grid=(lon_all // rows,),
        in_specs=[pl.BlockSpec((rows * members, band), lambda i: (i, 0))],
        out_specs=[pl.BlockSpec((rows, wide), lambda i: (i, 0))] * 2,
        scratch_shapes=[pltpu.VMEM((rows * members, band), F32)],
        cost_estimate=pl.CostEstimate(
            flops=perturbations.size, bytes_accessed=4 * perturbations.size, transcendentals=0
        ),
        compiler_params=pltpu.CompilerParams(vmem_limit_bytes=8 << 20),
        name="prepare_perturbations",
    )(perturbations.reshape(lon_all * members, band))


def prepare_controls_kernel(members, c_ref, out_ref, wide_ref):
    wide_ref[...] = c_ref[...].astype(F32)
    rows = out_ref.shape[1]
    for member in range(members):
        out_ref[member] = wide_ref[pl.ds(member, rows, stride=members), :].astype(BF16)


def prepare_controls(controls):
    lon_dev, members, lat_all = controls.shape
    lanes = 128
    return pl.pallas_call(
        functools.partial(prepare_controls_kernel, members),
        out_shape=jax.ShapeDtypeStruct((members, lon_dev, lat_all), BF16),
        grid=(lat_all // lanes,),
        in_specs=[pl.BlockSpec((lon_dev * members, lanes), lambda i: (0, i))],
        out_specs=pl.BlockSpec((members, lon_dev, lanes), lambda i: (0, 0, i)),
        scratch_shapes=[pltpu.VMEM((lon_dev * members, lanes), F32)],
        cost_estimate=pl.CostEstimate(
            flops=controls.size, bytes_accessed=4 * controls.size, transcendentals=0
        ),
        compiler_params=pltpu.CompilerParams(vmem_limit_bytes=8 << 20),
        name="prepare_controls",
    )(controls.reshape(lon_dev * members, lat_all))


def latitude_rows(place, parts, all_ref, blocks, out_ref, columns=None):
    me, part = place[0], place[1]
    piece = next(iter(parts.values()))[0].shape[0]
    narrow = piece // 2
    halves = sorted({h for _, h in blocks})
    for at, h in enumerate(halves):
        for s in range(4):
            start = (at * 4 + s) * piece
            all_ref[start : start + piece, :] = parts[h][s][...]
    for j, (s, h) in enumerate(blocks):
        d = me ^ s
        start = (halves.index(h) * 4 + ((d // 2) ^ part)) * piece + (d % 2) * narrow
        rows = pl.ds(pl.multiple_of(start, narrow), narrow)
        here = slice(j * narrow, (j + 1) * narrow)
        if columns is None:
            out_ref[here, :] = all_ref[rows, :]
        else:
            for i, t in enumerate(columns):
                lanes = pl.ds(pl.multiple_of((me ^ t) * 2 * narrow, 2 * narrow), 2 * narrow)
                out_ref[here, i * 2 * narrow : (i + 1) * 2 * narrow] = all_ref[rows, lanes]


def local_call(body, out_shape, scratch, flops, traffic, limit, out_spec=VMEM):
    outs = out_shape if isinstance(out_shape, list) else [out_shape]
    specs = [out_spec] * len(outs)

    def run(place, *args):
        return pl.pallas_call(
            body,
            out_shape=out_shape,
            in_specs=[pl.BlockSpec(memory_space=pltpu.SMEM)] + [VMEM] * len(args),
            out_specs=specs if isinstance(out_shape, list) else out_spec,
            scratch_shapes=scratch,
            cost_estimate=pl.CostEstimate(flops=flops, bytes_accessed=traffic, transcendentals=0),
            compiler_params=pltpu.CompilerParams(vmem_limit_bytes=limit << 20),
        )(place, *args)

    return run


def banded_kernel(halves, group, place, c_ref, *refs):
    count = 4 * len(halves)
    parts = {h: refs[4 * i : 4 * i + 4] for i, h in enumerate(halves)}
    out_refs = refs[count : count + len(group)]
    all_ref, rows_ref, turned_ref = refs[count + len(group) :]
    me = place[0]
    blocks = [(s, h) for s in group for h in halves]
    lanes = parts[halves[0]][0].shape[0]
    latitude_rows(place, parts, all_ref, blocks, rows_ref)
    turned_ref[...] = rows_ref[...].T
    members, rows, depth = c_ref.shape
    step = 256

    def body(pair, carry):
        left = c_ref[pl.ds(2 * pair, 2)].reshape(2 * rows, depth)
        to = pl.ds(pl.multiple_of(pair * lanes, lanes), lanes)
        for c in range(0, turned_ref.shape[1], step):
            product = jnp.dot(left, turned_ref[:, c : c + step], preferred_element_type=F32)
            for b in range(0, step, lanes):
                for i in range(2):
                    s, h = blocks[2 * (c + b) // lanes + i]
                    where = pl.ds(pl.multiple_of((me ^ s) * lanes, lanes), lanes)
                    own = pack(
                        c_ref[2 * pair, :, where].astype(F32),
                        c_ref[2 * pair + 1, :, where].astype(F32),
                        h,
                    )
                    term = pack(product[:rows, b : b + lanes], product[rows:, b : b + lanes], i)
                    out_refs[group.index(s)][halves.index(h), :, to] = (own + term).astype(BF16)
        return carry

    lax.fori_loop(0, members // 2, body, 0)


def banded(halves, group, place, c_members, lat):
    members, lon_dev, lat_all = c_members.shape
    piece = lat[0][0].shape[0]
    count, cut = len(group), len(halves)
    blocks = count * cut
    parts = [part for h in halves for part in lat[h]]
    return local_call(
        functools.partial(banded_kernel, halves, group),
        [jax.ShapeDtypeStruct((cut, lon_dev, members // 2 * piece), BF16)] * count,
        [
            pltpu.VMEM((len(parts) * piece, lat_all), BF16),
            pltpu.VMEM((blocks * piece // 2, lat_all), BF16),
            pltpu.VMEM((lat_all, blocks * piece // 2), BF16),
        ],
        lon_dev * members * lat_all * blocks * piece,
        2 * c_members.size + 2 * len(parts) * piece * lat_all,
        12,
    )(place, c_members, *parts)


def increment_kernel(half, place, *refs):
    moved, lon_refs, x_ref, outs = refs[:8], refs[8:12], refs[12], refs[13:15]
    columns, sum_ref = refs[15:]
    me, part = place[0], place[1]
    lon_dev, wide = moved[0].shape[1:]
    depth = lon_refs[0].shape[0]
    lanes = sum_ref.shape[2]
    for s in range(8):
        rows = pl.ds(pl.multiple_of((me ^ s) * lon_dev, lon_dev), lon_dev)
        columns[rows, :] = moved[s][half if moved[s].shape[0] > 1 else 0]
    step = 256
    for s in range(4):
        rows = pl.ds(pl.multiple_of((part ^ s) * depth, depth), depth)
        total = None
        for c in range(0, wide, step):
            local = jnp.dot(lon_refs[s][...], columns[:, c : c + step], preferred_element_type=F32)
            local = local + columns[rows, c : c + step].astype(F32)
            local = local * x_ref[rows, c : c + step].astype(F32)
            for b in range(0, step, lanes):
                term = local[:, b : b + lanes]
                total = term if total is None else total + term
        sum_ref[s] = total + swap(total)
    flip = jnp.where(low_lanes(outs[0].shape), 0, 1) == part // 2
    for ref, s in ((outs[0], 1), (outs[1], 0)):
        ref[...] = jnp.where(flip, sum_ref[s], sum_ref[s + 2])


def increment(half, place, moved, lon, x_packed):
    lon_all, wide = x_packed.shape
    depth = lon[0].shape[0]
    lanes = 128
    return local_call(
        functools.partial(increment_kernel, half),
        [jax.ShapeDtypeStruct((depth, lanes), F32)] * 2,
        [pltpu.VMEM((lon_all, wide), BF16), pltpu.VMEM((4, depth, lanes), F32)],
        2 * lon_all * lon_all * wide,
        2 * lon_all * lon_all + 4 * lon_all * wide,
        14,
    )(place, *moved, *lon, x_packed)


def weigh(place, grads, x_ref, weighted):
    part = place[1]
    depth, lanes = grads[0].shape
    wide = x_ref.shape[1]
    mark = jnp.where(low_lanes((depth, lanes)), 0, 1)
    for t in range(4):
        packed = grads[t % 2][...].astype(F32)
        both = jnp.where(mark == ((part // 2) ^ (t // 2)), packed, swap(packed))
        rows = pl.ds(pl.multiple_of((part ^ t) * depth, depth), depth)
        for b in range(0, wide, lanes):
            weighted[t * depth : (t + 1) * depth, b : b + lanes] = (
                x_ref[rows, b : b + lanes].astype(F32) * both
            ).astype(BF16)


def spread_kernel(group, first, place, *refs):
    if first:
        grads, x_ref, refs = refs[:2], refs[2], refs[3:]
        lon_refs, out_refs, weighted = refs[:4], refs[4:-1], refs[-1]
        weigh(place, grads, x_ref, weighted)
    else:
        weighted, lon_refs, out_refs = refs[0], refs[1:5], refs[5:]
    me, part = place[0], place[1]
    lon_dev = out_refs[0].shape[0]
    depth = lon_refs[0].shape[0]
    for j, s in enumerate(group):
        d = me ^ s
        columns = pl.ds(pl.multiple_of(d * lon_dev, lon_dev), lon_dev)
        start = ((d // 2) ^ part) * depth + (d % 2) * lon_dev
        total = weighted[pl.ds(pl.multiple_of(start, lon_dev), lon_dev), :].astype(F32)
        for t in range(4):
            total = total + lax.dot_general(
                lon_refs[t][:, columns],
                weighted[t * depth : (t + 1) * depth, :],
                (((0,), (0,)), ((), ())),
                preferred_element_type=F32,
            )
        out_refs[j][...] = total.astype(BF16)


def spread_back(group, first, place, inputs, lon, lon_dev):
    lon_all, wide = inputs[-1].shape
    count = len(group)
    block = jax.ShapeDtypeStruct((lon_dev, wide), BF16)
    outs = [block] * count + ([jax.ShapeDtypeStruct((lon_all, wide), BF16)] if first else [])
    return local_call(
        functools.partial(spread_kernel, group, first),
        outs,
        [],
        2 * lon_all * lon_dev * wide * count,
        2 * lon_all * lon_all + 4 * lon_all * wide,
        12,
    )(place, *inputs, *lon)


def contract_kernel(half, sources, members, last, place, base_ref, *refs):
    count = len(sources)
    messages, refs = refs[:count], refs[count:]
    parts, refs = {half: refs[:4]}, refs[4:]
    me = place[0]
    lanes = parts[half][0].shape[0]
    if last:
        out_hbm, all_ref, lat_ref, left_ref, stage_ref, out_sem = refs
    else:
        out_ref, all_ref, lat_ref, left_ref = refs
    latitude_rows(place, parts, all_ref, [(s, half) for s in sources], lat_ref, sources)
    rows = left_ref.shape[0] // members
    steps = base_ref.shape[1] // rows

    def copy_out(at, slot, i):
        start = pl.multiple_of(at * members * rows, members * rows)
        to_lanes = pl.ds(pl.multiple_of((me ^ sources[i]) * lanes, lanes), lanes)
        return pltpu.make_async_copy(
            stage_ref.at[slot, i],
            out_hbm.at[pl.ds(start, members * rows), to_lanes],
            out_sem.at[slot, i],
        )

    def body(step, carry):
        slot = step % 2
        here = pl.ds(pl.multiple_of(step * rows, rows), rows)
        if last:

            @pl.when(step >= 2)
            def _():
                for i in range(count):
                    copy_out(step - 2, slot, i).wait()

        def read(j, pair):
            return messages[j][here, pair * lanes : (pair + 1) * lanes].astype(F32)

        for member in range(members):
            for j in range(0, count, 2):
                both = pack(read(j, member // 2), read(j + 1, member // 2), member % 2)
                left_ref[
                    member * rows : (member + 1) * rows, j // 2 * lanes : (j // 2 + 1) * lanes
                ] = both.astype(BF16)
        wide = 256
        for c in range(0, count * lanes, wide):
            product = jnp.dot(left_ref[...], lat_ref[:, c : c + wide], preferred_element_type=F32)
            for b in range(0, wide, lanes):
                i = (c + b) // lanes
                where = pl.ds(pl.multiple_of((me ^ sources[i]) * lanes, lanes), lanes)
                for k in range(members):
                    value = product[k * rows : (k + 1) * rows, b : b + lanes]
                    packed = read(i, k // 2)
                    if half != k % 2:
                        packed = swap(packed)
                    mask = low_lanes(packed.shape)
                    zero = jnp.zeros_like(packed)
                    value = value + (
                        jnp.where(mask, zero, packed) if half else jnp.where(mask, packed, zero)
                    )
                    value = value + base_ref[k, here, where].astype(F32)
                    if last:
                        stage_ref[slot, i, pl.ds(k, rows, stride=members), :] = value
                    else:
                        out_ref[k, here, where] = value
                if last:
                    copy_out(step, slot, i).start()
        return carry

    lax.fori_loop(0, steps, body, 0)
    if last:
        for at in (steps - 2, steps - 1):
            for i in range(count):
                copy_out(at, at % 2, i).wait()


def contract(half, place, base, messages, lat, last):
    members, lon_dev, lat_all = base.shape
    sources = FAR + NEAR
    piece = lat[0][0].shape[0]
    rows = 64
    scratch = [
        pltpu.VMEM((4 * piece, lat_all), BF16),
        pltpu.VMEM((4 * piece, lat_all), BF16),
        pltpu.VMEM((members * rows, 4 * piece), BF16),
    ]
    if last:
        out_shape, out_spec = jax.ShapeDtypeStruct((lon_dev * members, lat_all), F32), ANY
        scratch += [
            pltpu.VMEM((2, len(sources), members * rows, piece), F32),
            pltpu.SemaphoreType.DMA((2, len(sources))),
        ]
    else:
        out_shape, out_spec = jax.ShapeDtypeStruct(base.shape, F32), VMEM
    return local_call(
        functools.partial(contract_kernel, half, sources, members, last),
        out_shape,
        scratch,
        members * lon_dev * lat_all * lat_all,
        8 * base.size,
        16,
        out_spec,
    )(place, base, *[messages[s] for s in sources], *lat[half])


def exchange(value, axis, size, shift):
    return lax.ppermute(value, axis, [(i, i ^ shift) for i in range(size)])


def local_fast(*args):
    return local_fast_body(*args)


def local_fast_body(controls, perturbations, lat_factor, lon_factor, obs_index, obs_weight, obs_count):
    lon_dev, members, lat_all = controls.shape
    lon_all, _, band = perturbations.shape
    narrow = band // 2
    part, me = lax.axis_index("mem"), lax.axis_index("lon")
    place = jnp.stack([me, part]).astype(jnp.int32)
    shard = lat_factor.shape[0]
    split = lat_factor.reshape(shard // band, 2, narrow, lat_all)

    def gathered(value):
        across = exchange(value, "mem", 4, 2)
        beside = exchange(value, "mem", 4, 1)
        return [value, beside, across, exchange(across, "mem", 4, 1)]

    lat = [gathered(split[:, h].reshape(shard // 2, lat_all)) for h in range(2)]
    lon = gathered(lon_factor)
    c_members = prepare_controls(controls)
    x_packed = prepare_perturbations(perturbations)
    own_map = weight_map(obs_index, obs_weight, obs_count, lon_all // 4, band)
    other_map = exchange(own_map, "mem", 4, 2)
    first_side = part < 2
    low_map = jnp.where(first_side, own_map, other_map)
    high_map = jnp.where(first_side, other_map, own_map)

    def sent(group, blocks):
        return {s: exchange(block, "lon", 8, s) if s else block for s, block in zip(group, blocks)}

    far = [sent(FAR, banded((h,), FAR, place, c_members, lat)) for h in range(2)]
    near = sent(NEAR, banded((0, 1), NEAR, place, c_members, lat))
    base = c_members
    for h in range(2):
        moved = [(far[h] | near)[s] for s in range(8)]
        send, keep = increment(h, place, moved, lon, x_packed[h])
        keep = keep + exchange(send, "mem", 4, 1)
        keep = keep + exchange(keep, "mem", 4, 2)
        cells = slice(h * narrow, (h + 1) * narrow)
        weights = jnp.concatenate([low_map[:, cells], high_map[:, cells]], axis=1)
        own = (keep * weights).astype(BF16)
        other = exchange(own, "mem", 4, 1)
        *blocks, weighted = spread_back(FAR, True, place, [own, other, x_packed[h]], lon, lon_dev)
        back = sent(FAR, blocks)
        blocks = spread_back(NEAR, False, place, [weighted], lon, lon_dev)
        back |= sent(NEAR, blocks)
        base = contract(h, place, base, back, lat, h == 1)
    return base.reshape(lon_dev, members, lat_all)


def local_plain(controls, perturbations, lat_factor, lon_factor, obs_index, obs_weight, obs_count):
    lon_dev, mem_dev, lat_all = controls.shape
    lat_full = lax.all_gather(lat_factor, "mem", axis=0, tiled=True)
    control_rows = controls.reshape(lon_dev * mem_dev, lat_all)
    band_rows = (
        control_rows.astype(F32)
        + lax.dot_general(
            control_rows, lat_full, (((1,), (1,)), ((), ())), preferred_element_type=F32
        )
    ).astype(BF16)
    moved = lax.all_to_all(
        band_rows.reshape(lon_dev, mem_dev, lat_all), "lon", split_axis=2, concat_axis=0, tiled=True
    )
    lon_all, _, lat_band = moved.shape
    columns = moved.reshape(lon_all, mem_dev * lat_band)
    lon_full = lax.all_gather(lon_factor, "mem", axis=0, tiled=True)
    localized = columns.astype(F32) + jnp.dot(lon_full, columns, preferred_element_type=F32)
    weighted_fwd = perturbations.reshape(lon_all, mem_dev * lat_band).astype(F32) * localized
    partial_sum = jnp.sum(weighted_fwd.reshape(lon_all, mem_dev, lat_band), axis=1)
    tile_sum = lax.psum_scatter(partial_sum, "mem", scatter_dimension=0, tiled=True)
    weights = weight_map(obs_index, obs_weight, obs_count, tile_sum.shape[0], lat_band)
    grad_tile = (tile_sum * weights).astype(BF16)
    gradient = lax.all_gather(grad_tile, "mem", axis=0, tiled=True)
    weighted = (
        (perturbations.astype(F32) * gradient.astype(F32)[:, None, :])
        .astype(BF16)
        .reshape(lon_all, mem_dev * lat_band)
    )
    back = lax.dot_general(
        lon_full, weighted, (((0,), (0,)), ((), ())), preferred_element_type=F32
    )
    spread = (weighted.astype(F32) + back).astype(BF16).reshape(lon_all, mem_dev, lat_band)
    returned = lax.all_to_all(spread, "lon", split_axis=0, concat_axis=2, tiled=True)
    back_rows = returned.reshape(lon_dev * mem_dev, lat_all)
    result = (
        control_rows.astype(F32)
        + back_rows.astype(F32)
        + jnp.dot(back_rows, lat_full, preferred_element_type=F32)
    )
    return result.reshape(lon_dev, mem_dev, lat_all)


def solution(mesh):
    in_specs = (
        P("lon", "mem", None),
        P(None, "mem", "lon"),
        P("mem", None),
        P("mem", None),
        P("mem", "lon", None),
        P("mem", "lon", None),
        P("mem", "lon"),
    )
    out_specs = P("lon", "mem", None)
    few = mesh.shape["mem"] == 4 and mesh.shape["lon"] == 8

    def local(controls, perturbations, lat_factor, *rest):
        lon_dev, members, _ = controls.shape
        lon_all, _, band = perturbations.shape
        fits = (
            few
            and band == 128
            and members == 8
            and lat_factor.shape[0] == 2 * band
            and lon_dev == 256
            and lon_all == 8 * lon_dev
        )
        plan = local_fast if fits else local_plain
        return plan(controls, perturbations, lat_factor, *rest)

    return jax.shard_map(local, mesh=mesh, in_specs=in_specs, out_specs=out_specs, check_vma=False)
```

time: 711 us -> 316 us (0.44)
  local copies, waits for them, and re-layouts: 218 us -> 4.26 us
  other arithmetic: 181 us -> 3.54 us
  blocking collectives: 106 us -> 0 us
  starting transfers between devices: 5.82 us -> 99.2 us
  Pallas kernels: 0 us -> 81.9 us
  matrix products: 49.4 us -> 0 us
  between operations: 13.8 us -> 1.12 us
  waiting for transfers between devices: 136 us -> 126 us
    gather x1 -> x0, local copies, waits for them, and re-layouts: 181 us -> none  [observe(): picked = flattened[where_at]]
    scatter-add x1 -> x0, other arithmetic: 171 us -> none  [observe(): return jnp.zeros_like(flattened).at[where_at.reshape(-1)].add(values.resh...]
    ppermute x0 -> x41, waiting for transfers between devices: none -> 126 us  [exchange(): return lax.ppermute(value, axis, [(i, i ^ shift) for i in range(size)])]
    all_to_all x1 -> x0, blocking collectives: 99.4 us -> none  [local(): lax.all_to_all(spread, 'lon', split_axis=0, concat_axis=2, tiled=True)]
    ppermute x0 -> x41, starting transfers between devices: none -> 99.2 us  [exchange(): return lax.ppermute(value, axis, [(i, i ^ shift) for i in range(size)])]
    all_to_all x1 -> x0, waiting for transfers between devices: 85.6 us -> none  [local(): lax.all_to_all(banded.reshape(lon_dev, mem_dev, lat_all), 'lon', split_ax...]
    pallas_call x0 -> x14, Pallas kernels: none -> 81.9 us  [the longest x11 63.1 us: run(): pl.pallas_call(body, out_shape=out_shape, in_specs=[pl.BlockSpec(memory_s...]
    dot_general x4 -> x0, matrix products: 49.4 us -> none  [the longest x1 17.6 us: local(): spread_fwd = jnp.dot(lon_full, columns, preferred_element_type=jnp.float32)]
  transfers between devices with their start and end apart: 4 -> 41, of which waited for: 3 -> 13; matrix products, arithmetic and copies ran while one was open for 5% -> 2% of each run, Pallas kernels for 0% -> 24%
where the time goes in v1:
time: 316 us
  waiting for transfers between devices  126 us (40%)
  starting transfers between devices  99.2 us (31%)
  Pallas kernels  81.9 us (26%)
  local copies, waits for them, and re-layouts  4.26 us (1%)
  other arithmetic  3.54 us (1%)
    ppermute x41, waiting for transfers between devices, exchange(): return lax.ppermute(value, axis, [(i, i ^ shift) for i in range(size)])  126 us
    ppermute x41, starting transfers between devices, exchange(): return lax.ppermute(value, axis, [(i, i ^ shift) for i in range(size)])  99.2 us
    pallas_call x11, Pallas kernels, run(): pl.pallas_call(body, out_shape=out_shape, in_specs=[pl.BlockSpec(memory_s...  63.1 us
    pallas_call x1, Pallas kernels, weight_map(): pl.pallas_call(functools.partial(weight_map_kernel, chunk, band), out_sha...  11.5 us
  transfers between devices with their start and end apart: 41, of which 13 were waited for; matrix products, arithmetic and copies ran while one was open for 2% of the time, Pallas kernels for 24%

profile of v1, /device:TPU:0, one launch (start us, length us, event | category | flops | bytes accessed | tf_op | source)
XLA Modules:
  0.0 315.5 jit_solution(15841869466886005514)
XLA Ops:
  0.0 3.0 collective-permute-start.14
  3.0 45.9 %collective-permute-done.14.refs_10_.refs_5_.refs_3_ = bf16[512,2048]{1,0:T(8,128)(2,1)} collective-permute-done((bf16[512,2048]{1,0:T(8,128)(2,1)}, bf16[512,2048]{1,0:T(8,128)(2,1)}, u32[]{:S(2)}, u32[]{:S(2)}) %collective-permute-start.14) | collective-permute-done | bytes 2097184 | tf_op jit(solution)/shard_map/ppermute | solution.py:434
  48.9 1.1 fusion.2
  50.0 1.8 collective-permute-start.4
  51.8 0.3 collective-permute-start.1
  52.1 7.1 %collective-permute-done.4.refs_6_.refs_2_.refs_10_ = bf16[128,1024]{1,0:T(8,128)(2,1)S(1)} collective-permute-done((bf16[128,1024]{1,0:T(8,128)(2,1)S(1)}, bf16[128,1024]{1,0:T(8,128)(2,1)S(1)}, u32[]{:S(2)}, u32[]{:S(2)}) %collective-permute-start.4) | collective-permute-done | bytes 262176 | tf_op jit(solution)/shard_map/ppermute | solution.py:434
  59.2 2.2 copy-done.3
  61.4 4.1 %prepare_controls.1.c_ref.base_ref = bf16[8,256,1024]{2,1,0:T(8,128)(2,1)S(1)} custom-call(bf16[2048,1024]{1,0:T(8,128)(2,1)S(1)} %bitcast.16), custom_call_target="tpu_custom_call" | custom-call | flops 2097152 | bytes 8388608 | tf_op jit(solution)/shard_map/prepare_controls/pallas_call | solution.py:125
  65.6 0.6 collective-permute-start
  66.3 2.9 shard_map.79
  69.2 2.9 collective-permute-start.27
  72.1 1.3 collective-permute-start.28
  73.4 3.6 %collective-permute-start.29 = (bf16[1,256,512]{2,1,0:T(8,128)(2,1)S(1)}, bf16[1,256,512]{2,1,0:T(8,128)(2,1)S(1)}, u32[]{:S(2)}, u32[]{:S(2)}) collective-permute-start(bf16[1,256,512]{2,1,0:T(8,128)(2,1)S(1)} %get-tuple-element.63), channel_id=1, source_target_pairs={{0,6},{1,7},{2,4},{3,5},{4,2},{5,3},{6,0},{7,1},{8,14},{9,15},{10,... | collective-permute-start | bytes 786440 | tf_op jit(solution)/shard_map/ppermute | solution.py:434
  77.0 19.2 %collective-permute-done.27.refs_4_ = bf16[1,256,512]{2,1,0:T(8,128)(2,1)S(1)} collective-permute-done((bf16[1,256,512]{2,1,0:T(8,128)(2,1)S(1)}, bf16[1,256,512]{2,1,0:T(8,128)(2,1)S(1)}, u32[]{:S(2)}, u32[]{:S(2)}) %collective-permute-start.27) | collective-permute-done | bytes 262176 | tf_op jit(solution)/shard_map/ppermute | solution.py:434
  96.2 4.2 %collective-permute-start.30 = (bf16[1,256,512]{2,1,0:T(8,128)(2,1)S(1)}, bf16[1,256,512]{2,1,0:T(8,128)(2,1)S(1)}, u32[]{:S(2)}, u32[]{:S(2)}) collective-permute-start(bf16[1,256,512]{2,1,0:T(8,128)(2,1)S(1)} %get-tuple-element.64), channel_id=1, source_target_pairs={{0,7},{1,6},{2,5},{3,4},{4,3},{5,2},{6,1},{7,0},{8,15},{9,14},{10,... | collective-permute-start | bytes 786440 | tf_op jit(solution)/shard_map/ppermute | solution.py:434
  101.0 3.2 %prepare_perturbations.1 = (bf16[2048,512]{1,0:T(8,128)(2,1)S(1)}, bf16[2048,512]{1,0:T(8,128)(2,1)S(1)}) custom-call(bf16[16384,128]{1,0:T(8,128)(2,1)S(1)} %bitcast.17), custom_call_target="tpu_custom_call" | custom-call | flops 2097152 | bytes 8388608 | tf_op jit(solution)/shard_map/prepare_perturbations/pallas_call | solution.py:100
  104.3 4.7 %shard_map.73 = (bf16[2,256,512]{2,1,0:T(8,128)(2,1)S(1)}, bf16[2,256,512]{2,1,0:T(8,128)(2,1)S(1)}, bf16[2,256,512]{2,1,0:T(8,128)(2,1)S(1)}, bf16[2,256,512]{2,1,0:T(8,128)(2,1)S(1)}) custom-call(s32[2]{0:T(128)S(1)} %pad_add_fusion.place, bf16[8,256,1024]{2,1,0:T(8,128)(2,1)S(1)} %prepare_controls.1.c_ref.base_ref, bf16[128,1024]{1,0:T(8,128)(2,1)S(1)} %bitcast.25, ...), custom_call_target="tpu_custom_call" | custom-call | flops 2147483648 | bytes 6291456 | tf_op jit(solution)/shard_map/pallas_call | solution.py:167
  109.0 0.6 collective-permute-start.6
  109.6 4.0 %collective-permute-start.7 = (bf16[2,256,512]{2,1,0:T(8,128)(2,1)S(1)}, bf16[2,256,512]{2,1,0:T(8,128)(2,1)S(1)}, u32[]{:S(2)}, u32[]{:S(2)}) collective-permute-start(bf16[2,256,512]{2,1,0:T(8,128)(2,1)S(1)} %get-tuple-element.43), channel_id=1, source_target_pairs={{0,2},{1,3},{2,0},{3,1},{4,6},{5,7},{6,4},{7,5},{8,10},{9,11},{10,... | collective-permute-start | bytes 1572872 | tf_op jit(solution)/shard_map/ppermute | solution.py:434
  113.6 6.4 %collective-permute-start.8 = (bf16[2,256,512]{2,1,0:T(8,128)(2,1)S(1)}, bf16[2,256,512]{2,1,0:T(8,128)(2,1)S(1)}, u32[]{:S(2)}, u32[]{:S(2)}) collective-permute-start(bf16[2,256,512]{2,1,0:T(8,128)(2,1)S(1)} %get-tuple-element.44), channel_id=1, source_target_pairs={{0,3},{1,2},{2,1},{3,0},{4,7},{5,6},{6,5},{7,4},{8,11},{9,10},{10,... | collective-permute-start | bytes 1572872 | tf_op jit(solution)/shard_map/ppermute | solution.py:434
  120.0 11.5 %weight_map.1 = f32[512,128]{1,0:T(8,128)} custom-call(s32[1]{0:T(128)} %bitcast.15.count_ref, s32[1,32768]{1,0:T(1,128)S(1)} %bitcast.28, f32[1,32768]{1,0:T(1,128)S(1)} %bitcast.29), custom_call_target="tpu_custom_call" | custom-call | flops 8589934592 | bytes 262144 | tf_op jit(solution)/shard_map/weight_map/pallas_call | solution.py:48
  131.5 3.1 shard_map.74
  134.6 1.6 collective-permute-start.18
  136.1 2.0 collective-permute-start.9
  138.1 3.3 %collective-permute-start.10 = (bf16[1,256,512]{2,1,0:T(8,128)(2,1)S(1)}, bf16[1,256,512]{2,1,0:T(8,128)(2,1)S(1)}, u32[]{:S(2)}, u32[]{:S(2)}) collective-permute-start(bf16[1,256,512]{2,1,0:T(8,128)(2,1)S(1)} %get-tuple-element.46), channel_id=1, source_target_pairs={{0,5},{1,4},{2,7},{3,6},{4,1},{5,0},{6,3},{7,2},{8,13},{9,12},{10,... | collective-permute-start | bytes 786440 | tf_op jit(solution)/shard_map/ppermute | solution.py:434
  141.4 2.0 collective-permute-start.11
  143.4 2.8 collective-permute-start.12
  146.2 8.4 %shard_map.80 = (f32[512,128]{1,0:T(8,128)}, f32[512,128]{1,0:T(8,128)S(1)}) custom-call(s32[2]{0:T(128)S(1)} %pad_add_fusion.place, bf16[2,256,512]{2,1,0:T(8,128)(2,1)S(1)} %get-tuple-element.41.refs_0_, bf16[2,256,512]{2,1,0:T(8,128)(2,1)S(1)} %collective-permute-done.6.refs_1_, bf16[2,256,512]{2,1,0:T(8,128)(2,1)S(1)} %collective-permute-done.7.refs_2_, ...), custom_call_target="tpu_custom_call" | custom-call | flops 4294967296 | bytes 12582912 | tf_op jit(solution)/shard_map/pallas_call | solution.py:167
  154.6 13.4 %collective-permute-done.9.refs_4_ = bf16[1,256,512]{2,1,0:T(8,128)(2,1)S(1)} collective-permute-done((bf16[1,256,512]{2,1,0:T(8,128)(2,1)S(1)}, bf16[1,256,512]{2,1,0:T(8,128)(2,1)S(1)}, u32[]{:S(2)}, u32[]{:S(2)}) %collective-permute-start.9) | collective-permute-done | bytes 262176 | tf_op jit(solution)/shard_map/ppermute | solution.py:434
  168.1 6.6 %collective-permute-done.10.refs_5_ = bf16[1,256,512]{2,1,0:T(8,128)(2,1)S(1)} collective-permute-done((bf16[1,256,512]{2,1,0:T(8,128)(2,1)S(1)}, bf16[1,256,512]{2,1,0:T(8,128)(2,1)S(1)}, u32[]{:S(2)}, u32[]{:S(2)}) %collective-permute-start.10) | collective-permute-done | bytes 262176 | tf_op jit(solution)/shard_map/ppermute | solution.py:434
  174.6 8.5 %shard_map.75 = (f32[512,128]{1,0:T(8,128)}, f32[512,128]{1,0:T(8,128)S(1)}) custom-call(s32[2]{0:T(128)S(1)} %pad_add_fusion.place, bf16[2,256,512]{2,1,0:T(8,128)(2,1)S(1)} %get-tuple-element.41.refs_0_, bf16[2,256,512]{2,1,0:T(8,128)(2,1)S(1)} %collective-permute-done.6.refs_1_, bf16[2,256,512]{2,1,0:T(8,128)(2,1)S(1)} %collective-permute-done.7.refs_2_, ...), custom_call_target="tpu_custom_call" | custom-call | flops 4294967296 | bytes 12582912 | tf_op jit(solution)/shard_map/pallas_call | solution.py:167
  183.1 0.7 copy-done.17
  183.8 1.1 broadcast_select_fusion.1
  184.9 1.1 add.14
  186.0 0.8 collective-permute-start.32
  186.8 1.1 add.12
  187.8 1.3 collective-permute-start.17
  189.2 0.2 fusion.3
  189.4 11.0 %collective-permute-done.17 = f32[512,128]{1,0:T(8,128)S(1)} collective-permute-done((f32[512,128]{1,0:T(8,128)S(1)}, f32[512,128]{1,0:T(8,128)S(1)}, u32[]{:S(2)}, u32[]{:S(2)}) %collective-permute-start.17) | collective-permute-done | bytes 262176 | tf_op jit(solution)/shard_map/ppermute | solution.py:434
  200.8 0.6 collective-permute-start.33
  201.3 0.6 collective-permute-done.19.refs_1_
  201.9 5.8 %shard_map.76 = (bf16[256,512]{1,0:T(8,128)(2,1)S(1)}, bf16[256,512]{1,0:T(8,128)(2,1)S(1)}, bf16[256,512]{1,0:T(8,128)(2,1)S(1)}, bf16[256,512]{1,0:T(8,128)(2,1)S(1)}, bf16[2048,512]{1,0:T(8,128)(2,1)S(1)}) custom-call(s32[2]{0:T(128)S(1)} %pad_add_fusion.place, bf16[512,128]{1,0:T(8,128)(2,1)S(1)} %fusion.refs_0_, ...), custom_call_target="tpu_custom_call" | custom-call | flops 2147483648 | bytes 12582912 | tf_op jit(solution)/shard_map/pallas_call | solution.py:167
  207.7 2.3 collective-permute-start.20
  210.0 1.5 collective-permute-start.21
  211.5 10.7 %collective-permute-start.22 = (bf16[256,512]{1,0:T(8,128)(2,1)S(1)}, bf16[256,512]{1,0:T(8,128)(2,1)S(1)}, u32[]{:S(2)}, u32[]{:S(2)}) collective-permute-start(bf16[256,512]{1,0:T(8,128)(2,1)S(1)} %get-tuple-element.54), channel_id=1, source_target_pairs={{0,5},{1,4},{2,7},{3,6},{4,1},{5,0},{6,3},{7,2},{8,13},{9,12},{10,... | collective-permute-start | bytes 786440 | tf_op jit(solution)/shard_map/ppermute | solution.py:434
  222.3 6.0 %shard_map.81 = (bf16[256,512]{1,0:T(8,128)(2,1)S(1)}, bf16[256,512]{1,0:T(8,128)(2,1)S(1)}, bf16[256,512]{1,0:T(8,128)(2,1)S(1)}, bf16[256,512]{1,0:T(8,128)(2,1)S(1)}, bf16[2048,512]{1,0:T(8,128)(2,1)S(1)}) custom-call(s32[2]{0:T(128)S(1)} %pad_add_fusion.place, bf16[512,128]{1,0:T(8,128)(2,1)S(1)} %fusion.1.refs_0_, ...), custom_call_target="tpu_custom_call" | custom-call | flops 2147483648 | bytes 12582912 | tf_op jit(solution)/shard_map/pallas_call | solution.py:167
  228.3 1.9 collective-permute-start.34
  230.2 5.3 %shard_map.77 = (bf16[256,512]{1,0:T(8,128)(2,1)S(1)}, bf16[256,512]{1,0:T(8,128)(2,1)S(1)}, bf16[256,512]{1,0:T(8,128)(2,1)S(1)}, bf16[256,512]{1,0:T(8,128)(2,1)S(1)}) custom-call(s32[2]{0:T(128)S(1)} %pad_add_fusion.place, bf16[2048,512]{1,0:T(8,128)(2,1)S(1)} %get-tuple-element.56.refs_0_, bf16[512,2048]{1,0:T(8,128)(2,1)S(1)} %copy-done.2, ...), custom_call_target="tpu_custom_call" | custom-call | flops 2147483648 | bytes 12582912 | tf_op jit(solution)/shard_map/pallas_call | solution.py:167
  235.5 3.0 collective-permute-start.35
  238.5 20.3 %collective-permute-start.24 = (bf16[256,512]{1,0:T(8,128)(2,1)S(1)}, bf16[256,512]{1,0:T(8,128)(2,1)S(1)}, u32[]{:S(2)}, u32[]{:S(2)}) collective-permute-start(bf16[256,512]{1,0:T(8,128)(2,1)S(1)} %get-tuple-element.57), channel_id=1, source_target_pairs={{0,3},{1,2},{2,1},{3,0},{4,7},{5,6},{6,5},{7,4},{8,11},{9,10},{10,... | collective-permute-start | bytes 786440 | tf_op jit(solution)/shard_map/ppermute | solution.py:434
  258.8 5.2 %collective-permute-done.22.refs_2_ = bf16[256,512]{1,0:T(8,128)(2,1)S(1)} collective-permute-done((bf16[256,512]{1,0:T(8,128)(2,1)S(1)}, bf16[256,512]{1,0:T(8,128)(2,1)S(1)}, u32[]{:S(2)}, u32[]{:S(2)}) %collective-permute-start.22) | collective-permute-done | bytes 262176 | tf_op jit(solution)/shard_map/ppermute | solution.py:434
  263.9 4.6 %collective-permute-done.23.refs_3_ = bf16[256,512]{1,0:T(8,128)(2,1)S(1)} collective-permute-done((bf16[256,512]{1,0:T(8,128)(2,1)S(1)}, bf16[256,512]{1,0:T(8,128)(2,1)S(1)}, u32[]{:S(2)}, u32[]{:S(2)}) %collective-permute-start.23) | collective-permute-done | bytes 262176 | tf_op jit(solution)/shard_map/ppermute | solution.py:434
  268.5 1.5 collective-permute-start.26
  270.1 5.4 %shard_map.82 = (bf16[256,512]{1,0:T(8,128)(2,1)S(1)}, bf16[256,512]{1,0:T(8,128)(2,1)S(1)}, bf16[256,512]{1,0:T(8,128)(2,1)S(1)}, bf16[256,512]{1,0:T(8,128)(2,1)S(1)}) custom-call(s32[2]{0:T(128)S(1)} %pad_add_fusion.place, bf16[2048,512]{1,0:T(8,128)(2,1)S(1)} %get-tuple-element.72.refs_0_, bf16[512,2048]{1,0:T(8,128)(2,1)S(1)} %copy-done.2, ...), custom_call_target="tpu_custom_call" | custom-call | flops 2147483648 | bytes 12582912 | tf_op jit(solution)/shard_map/pallas_call | solution.py:167
  275.5 1.0 collective-permute-start.36
  276.5 10.3 %collective-permute-start.37 = (bf16[256,512]{1,0:T(8,128)(2,1)S(1)}, bf16[256,512]{1,0:T(8,128)(2,1)S(1)}, u32[]{:S(2)}, u32[]{:S(2)}) collective-permute-start(bf16[256,512]{1,0:T(8,128)(2,1)S(1)} %get-tuple-element.71), channel_id=1, source_target_pairs={{0,4},{1,5},{2,6},{3,7},{4,0},{5,1},{6,2},{7,3},{8,12},{9,13},{10,... | collective-permute-start | bytes 786440 | tf_op jit(solution)/shard_map/ppermute | solution.py:434
  286.9 1.9 collective-permute-start.39
  288.9 1.5 collective-permute-start.40
  290.4 5.7 %shard_map.78.base_ref = f32[8,256,1024]{2,1,0:T(8,128)S(1)} custom-call(s32[2]{0:T(128)S(1)} %pad_add_fusion.place, bf16[8,256,1024]{2,1,0:T(8,128)(2,1)S(1)} %copy-done.1, bf16[256,512]{1,0:T(8,128)(2,1)S(1)} %collective-permute-done.20.refs_0_, bf16[256,512]{1,0:T(8,128)(2,1)S(1)} %collective-permute-done.21.refs_1_, ...), custom_call_target="tpu_custom_call" | custom-call | flops 2147483648 | bytes 16777216 | tf_op jit(solution)/shard_map/pallas_call | solution.py:167
  296.1 1.6 collective-permute-done.36.refs_2_
  297.7 4.6 %collective-permute-done.37.refs_3_ = bf16[256,512]{1,0:T(8,128)(2,1)S(1)} collective-permute-done((bf16[256,512]{1,0:T(8,128)(2,1)S(1)}, bf16[256,512]{1,0:T(8,128)(2,1)S(1)}, u32[]{:S(2)}, u32[]{:S(2)}) %collective-permute-start.37) | collective-permute-done | bytes 262176 | tf_op jit(solution)/shard_map/ppermute | solution.py:434
  302.3 2.3 collective-permute-done.38.refs_4_
  304.6 3.4 %collective-permute-done.39.refs_5_ = bf16[256,512]{1,0:T(8,128)(2,1)S(1)} collective-permute-done((bf16[256,512]{1,0:T(8,128)(2,1)S(1)}, bf16[256,512]{1,0:T(8,128)(2,1)S(1)}, u32[]{:S(2)}, u32[]{:S(2)}) %collective-permute-start.39) | collective-permute-done | bytes 262176 | tf_op jit(solution)/shard_map/ppermute | solution.py:434
  308.0 7.4 %shard_map.83 = f32[2048,1024]{1,0:T(8,128)} custom-call(s32[2]{0:T(128)S(1)} %pad_add_fusion.place, f32[8,256,1024]{2,1,0:T(8,128)S(1)} %shard_map.78.base_ref, bf16[256,512]{1,0:T(8,128)(2,1)S(1)} %collective-permute-done.34.refs_0_, bf16[256,512]{1,0:T(8,128)(2,1)S(1)} %collective-permute-done.35.refs_1_, ...), custom_call_target="tpu_custom_call" | custom-call | flops 2147483648 | bytes 16777216 | tf_op jit(solution)/shard_map/pallas_call | solution.py:167
  (80 shorter events, 0.8 us)
Async XLA Ops:
  0.0 48.9 %collective-permute-start.14 = (bf16[512,2048]{1,0:T(8,128)(2,1)}, bf16[512,2048]{1,0:T(8,128)(2,1)}, u32[]{:S(2)}, u32[]{:S(2)}) collective-permute-start(bf16[512,2048]{1,0:T(8,128)(2,1)} %refs_1_.3), channel_id=1, source_target_pairs={{0,16},{8,24},{16,0},{24,8},{1,17},{9,25},{17,1},{25,9},{2,18},{10... | collective-permute-start | bytes 6291464 | tf_op jit(solution)/shard_map/ppermute | solution.py:434
  3.0 138.4 %collective-permute-start.13 = (bf16[512,2048]{1,0:T(8,128)(2,1)}, bf16[512,2048]{1,0:T(8,128)(2,1)}, u32[]{:S(2)}, u32[]{:S(2)}) collective-permute-start(bf16[512,2048]{1,0:T(8,128)(2,1)} %refs_1_.3), channel_id=1, source_target_pairs={{0,8},{8,0},{16,24},{24,16},{1,9},{9,1},{17,25},{25,17},{2,10},{10... | collective-permute-start | bytes 6291464 | tf_op jit(solution)/shard_map/ppermute | solution.py:434
  48.9 94.5 %collective-permute-start.15 = (bf16[512,2048]{1,0:T(8,128)(2,1)}, bf16[512,2048]{1,0:T(8,128)(2,1)}, u32[]{:S(2)}, u32[]{:S(2)}) collective-permute-start(bf16[512,2048]{1,0:T(8,128)(2,1)} %collective-permute-done.14.refs_10_.refs_5_.refs_3_), channel_id=1, source_target_pairs={{0,8},{8,0},{16,24},{24,16},{1,9},{9,1},{17,25},{25,17},{2,10},{10... | collective-permute-start | bytes 6291464 | tf_op jit(solution)/shard_map/ppermute | solution.py:434
  50.0 9.2 %collective-permute-start.4 = (bf16[128,1024]{1,0:T(8,128)(2,1)S(1)}, bf16[128,1024]{1,0:T(8,128)(2,1)S(1)}, u32[]{:S(2)}, u32[]{:S(2)}) collective-permute-start(bf16[128,1024]{1,0:T(8,128)(2,1)S(1)} %bitcast.18), channel_id=1, source_target_pairs={{0,16},{8,24},{16,0},{24,8},{1,17},{9,25},{17,1},{25,9},{2,18},{10... | collective-permute-start | bytes 786440 | tf_op jit(solution)/shard_map/ppermute | solution.py:434
  51.8 13.8 %collective-permute-start.1 = (bf16[128,1024]{1,0:T(8,128)(2,1)S(1)}, bf16[128,1024]{1,0:T(8,128)(2,1)S(1)}, u32[]{:S(2)}, u32[]{:S(2)}) collective-permute-start(bf16[128,1024]{1,0:T(8,128)(2,1)S(1)} %bitcast.23), channel_id=1, source_target_pairs={{0,16},{8,24},{16,0},{24,8},{1,17},{9,25},{17,1},{25,9},{2,18},{10... | collective-permute-start | bytes 786440 | tf_op jit(solution)/shard_map/ppermute | solution.py:434
  52.1 14.1 %collective-permute-start.3 = (bf16[128,1024]{1,0:T(8,128)(2,1)S(1)}, bf16[128,1024]{1,0:T(8,128)(2,1)S(1)}, u32[]{:S(2)}, u32[]{:S(2)}) collective-permute-start(bf16[128,1024]{1,0:T(8,128)(2,1)S(1)} %bitcast.19), channel_id=1, source_target_pairs={{0,8},{8,0},{16,24},{24,16},{1,9},{9,1},{17,25},{25,17},{2,10},{10... | collective-permute-start | bytes 786440 | tf_op jit(solution)/shard_map/ppermute | solution.py:434
  59.2 7.1 %collective-permute-start.5 = (bf16[128,1024]{1,0:T(8,128)(2,1)S(1)}, bf16[128,1024]{1,0:T(8,128)(2,1)S(1)}, u32[]{:S(2)}, u32[]{:S(2)}) collective-permute-start(bf16[128,1024]{1,0:T(8,128)(2,1)S(1)} %collective-permute-done.4.refs_6_.refs_2_.refs_10_), channel_id=1, source_target_pairs={{0,8},{8,0},{16,24},{24,16},{1,9},{9,1},{17,25},{25,17},{2,10},{10... | collective-permute-start | bytes 786440 | tf_op jit(solution)/shard_map/ppermute | solution.py:434
  59.2 2.2 copy-start.3
  65.5 66.0 %copy-start = (bf16[8,256,1024]{2,1,0:T(8,128)(2,1)}, bf16[8,256,1024]{2,1,0:T(8,128)(2,1)S(1)}, u32[]{:S(2)}) copy-start(bf16[8,256,1024]{2,1,0:T(8,128)(2,1)S(1)} %prepare_controls.1.c_ref.base_ref) | copy-start | bytes 12582916
  65.6 35.4 %copy-start.4 = (bf16[2048,8,128]{2,1,0:T(8,128)(2,1)S(1)}, bf16[2048,8,128]{2,1,0:T(8,128)(2,1)}, u32[]{:S(2)}) copy-start(bf16[2048,8,128]{2,1,0:T(8,128)(2,1)} %param.8) | copy-start | bytes 12582916
  65.6 38.6 %copy-start.9 = (bf16[128,1024]{1,0:T(8,128)(2,1)}, bf16[128,1024]{1,0:T(8,128)(2,1)S(1)}, u32[]{:S(2)}) copy-start(bf16[128,1024]{1,0:T(8,128)(2,1)S(1)} %collective-permute-done.1.refs_2_.refs_10_) | copy-start | bytes 786436
  65.6 6.4 %collective-permute-start = (bf16[128,1024]{1,0:T(8,128)(2,1)S(1)}, bf16[128,1024]{1,0:T(8,128)(2,1)S(1)}, u32[]{:S(2)}, u32[]{:S(2)}) collective-permute-start(bf16[128,1024]{1,0:T(8,128)(2,1)S(1)} %bitcast.24), channel_id=1, source_target_pairs={{0,8},{8,0},{16,24},{24,16},{1,9},{9,1},{17,25},{25,17},{2,10},{10... | collective-permute-start | bytes 786440 | tf_op jit(solution)/shard_map/ppermute | solution.py:434
  66.2 7.2 %collective-permute-start.2 = (bf16[128,1024]{1,0:T(8,128)(2,1)S(1)}, bf16[128,1024]{1,0:T(8,128)(2,1)S(1)}, u32[]{:S(2)}, u32[]{:S(2)}) collective-permute-start(bf16[128,1024]{1,0:T(8,128)(2,1)S(1)} %collective-permute-done.1.refs_2_.refs_10_), channel_id=1, source_target_pairs={{0,8},{8,0},{16,24},{24,16},{1,9},{9,1},{17,25},{25,17},{2,10},{10... | collective-permute-start | bytes 786440 | tf_op jit(solution)/shard_map/ppermute | solution.py:434
  69.2 27.0 %collective-permute-start.27 = (bf16[1,256,512]{2,1,0:T(8,128)(2,1)S(1)}, bf16[1,256,512]{2,1,0:T(8,128)(2,1)S(1)}, u32[]{:S(2)}, u32[]{:S(2)}) collective-permute-start(bf16[1,256,512]{2,1,0:T(8,128)(2,1)S(1)} %get-tuple-element.61), channel_id=1, source_target_pairs={{0,4},{1,5},{2,6},{3,7},{4,0},{5,1},{6,2},{7,3},{8,12},{9,13},{10,... | collective-permute-start | bytes 786440 | tf_op jit(solution)/shard_map/ppermute | solution.py:434
  72.1 59.4 %copy-start.12 = (bf16[128,1024]{1,0:T(8,128)(2,1)}, bf16[128,1024]{1,0:T(8,128)(2,1)S(1)}, u32[]{:S(2)}) copy-start(bf16[128,1024]{1,0:T(8,128)(2,1)S(1)} %collective-permute-done.refs_1_.refs_9_) | copy-start | bytes 786436
  72.1 37.0 %collective-permute-start.28 = (bf16[1,256,512]{2,1,0:T(8,128)(2,1)S(1)}, bf16[1,256,512]{2,1,0:T(8,128)(2,1)S(1)}, u32[]{:S(2)}, u32[]{:S(2)}) collective-permute-start(bf16[1,256,512]{2,1,0:T(8,128)(2,1)S(1)} %get-tuple-element.62), channel_id=1, source_target_pairs={{0,5},{1,4},{2,7},{3,6},{4,1},{5,0},{6,3},{7,2},{8,13},{9,12},{10,... | collective-permute-start | bytes 786440 | tf_op jit(solution)/shard_map/ppermute | solution.py:434
  73.4 58.1 %copy-start.14 = (bf16[128,1024]{1,0:T(8,128)(2,1)}, bf16[128,1024]{1,0:T(8,128)(2,1)S(1)}, u32[]{:S(2)}) copy-start(bf16[128,1024]{1,0:T(8,128)(2,1)S(1)} %collective-permute-done.2.refs_3_.refs_11_) | copy-start | bytes 786436
  73.4 36.2 %collective-permute-start.29 = (bf16[1,256,512]{2,1,0:T(8,128)(2,1)S(1)}, bf16[1,256,512]{2,1,0:T(8,128)(2,1)S(1)}, u32[]{:S(2)}, u32[]{:S(2)}) collective-permute-start(bf16[1,256,512]{2,1,0:T(8,128)(2,1)S(1)} %get-tuple-element.63), channel_id=1, source_target_pairs={{0,6},{1,7},{2,4},{3,5},{4,2},{5,3},{6,0},{7,1},{8,14},{9,15},{10,... | collective-permute-start | bytes 786440 | tf_op jit(solution)/shard_map/ppermute | solution.py:434
  96.2 17.4 %collective-permute-start.30 = (bf16[1,256,512]{2,1,0:T(8,128)(2,1)S(1)}, bf16[1,256,512]{2,1,0:T(8,128)(2,1)S(1)}, u32[]{:S(2)}, u32[]{:S(2)}) collective-permute-start(bf16[1,256,512]{2,1,0:T(8,128)(2,1)S(1)} %get-tuple-element.64), channel_id=1, source_target_pairs={{0,7},{1,6},{2,5},{3,4},{4,3},{5,2},{6,1},{7,0},{8,15},{9,14},{10,... | collective-permute-start | bytes 786440 | tf_op jit(solution)/shard_map/ppermute | solution.py:434
  104.3 41.9 %copy-start.5 = (bf16[2048,512]{1,0:T(8,128)(2,1)}, bf16[2048,512]{1,0:T(8,128)(2,1)S(1)}, u32[]{:S(2)}) copy-start(bf16[2048,512]{1,0:T(8,128)(2,1)S(1)} %get-tuple-element.65.refs_12_.refs_2_) | copy-start | bytes 6291460
  104.3 70.4 %copy-start.7 = (bf16[2048,512]{1,0:T(8,128)(2,1)}, bf16[2048,512]{1,0:T(8,128)(2,1)S(1)}, u32[]{:S(2)}) copy-start(bf16[2048,512]{1,0:T(8,128)(2,1)S(1)} %get-tuple-element.49.refs_12_.refs_2_) | copy-start | bytes 6291460
  104.3 15.7 %copy-start.18 = (s32[1,1,32768]{2,1,0:T(1,128)S(1)}, s32[1,1,32768]{2,1,0:T(1,128)}, u32[]{:S(2)}) copy-start(s32[1,1,32768]{2,1,0:T(1,128)} %param.11) | copy-start | bytes 393220
  104.3 15.7 %copy-start.19 = (f32[1,1,32768]{2,1,0:T(1,128)S(1)}, f32[1,1,32768]{2,1,0:T(1,128)}, u32[]{:S(2)}) copy-start(f32[1,1,32768]{2,1,0:T(1,128)} %param.12) | copy-start | bytes 393220
  109.0 25.5 %collective-permute-start.6 = (bf16[2,256,512]{2,1,0:T(8,128)(2,1)S(1)}, bf16[2,256,512]{2,1,0:T(8,128)(2,1)S(1)}, u32[]{:S(2)}, u32[]{:S(2)}) collective-permute-start(bf16[2,256,512]{2,1,0:T(8,128)(2,1)S(1)} %get-tuple-element.42), channel_id=1, source_target_pairs={{0,1},{1,0},{2,3},{3,2},{4,5},{5,4},{6,7},{7,6},{8,9},{9,8},{10,11... | collective-permute-start | bytes 1572872 | tf_op jit(solution)/shard_map/ppermute | solution.py:434
  109.6 26.5 %collective-permute-start.7 = (bf16[2,256,512]{2,1,0:T(8,128)(2,1)S(1)}, bf16[2,256,512]{2,1,0:T(8,128)(2,1)S(1)}, u32[]{:S(2)}, u32[]{:S(2)}) collective-permute-start(bf16[2,256,512]{2,1,0:T(8,128)(2,1)S(1)} %get-tuple-element.43), channel_id=1, source_target_pairs={{0,2},{1,3},{2,0},{3,1},{4,6},{5,7},{6,4},{7,5},{8,10},{9,11},{10,... | collective-permute-start | bytes 1572872 | tf_op jit(solution)/shard_map/ppermute | solution.py:434
  113.6 24.5 %collective-permute-start.8 = (bf16[2,256,512]{2,1,0:T(8,128)(2,1)S(1)}, bf16[2,256,512]{2,1,0:T(8,128)(2,1)S(1)}, u32[]{:S(2)}, u32[]{:S(2)}) collective-permute-start(bf16[2,256,512]{2,1,0:T(8,128)(2,1)S(1)} %get-tuple-element.44), channel_id=1, source_target_pairs={{0,3},{1,2},{2,1},{3,0},{4,7},{5,6},{6,5},{7,4},{8,11},{9,10},{10,... | collective-permute-start | bytes 1572872 | tf_op jit(solution)/shard_map/ppermute | solution.py:434
  120.0 11.5 %copy-start.10 = (bf16[128,1024]{1,0:T(8,128)(2,1)S(1)}, bf16[128,1024]{1,0:T(8,128)(2,1)}, u32[]{:S(2)}) copy-start(bf16[128,1024]{1,0:T(8,128)(2,1)} %copy-done.9) | copy-start | bytes 786436
  131.5 14.7 %copy-start.2 = (bf16[512,2048]{1,0:T(8,128)(2,1)S(1)}, bf16[512,2048]{1,0:T(8,128)(2,1)}, u32[]{:S(2)}) copy-start(bf16[512,2048]{1,0:T(8,128)(2,1)} %refs_1_.3) | copy-start | bytes 6291460
  134.6 49.3 %collective-permute-start.18 = (f32[512,128]{1,0:T(8,128)}, f32[512,128]{1,0:T(8,128)}, u32[]{:S(2)}, u32[]{:S(2)}) collective-permute-start(f32[512,128]{1,0:T(8,128)} %weight_map.1), channel_id=1, source_target_pairs={{0,16},{8,24},{16,0},{24,8},{1,17},{9,25},{17,1},{25,9},{2,18},{10... | collective-permute-start | bytes 786440 | tf_op jit(solution)/shard_map/ppermute | solution.py:434
  136.1 31.9 %collective-permute-start.9 = (bf16[1,256,512]{2,1,0:T(8,128)(2,1)S(1)}, bf16[1,256,512]{2,1,0:T(8,128)(2,1)S(1)}, u32[]{:S(2)}, u32[]{:S(2)}) collective-permute-start(bf16[1,256,512]{2,1,0:T(8,128)(2,1)S(1)} %get-tuple-element.45), channel_id=1, source_target_pairs={{0,4},{1,5},{2,6},{3,7},{4,0},{5,1},{6,2},{7,3},{8,12},{9,13},{10,... | collective-permute-start | bytes 786440 | tf_op jit(solution)/shard_map/ppermute | solution.py:434
  138.1 36.5 %collective-permute-start.10 = (bf16[1,256,512]{2,1,0:T(8,128)(2,1)S(1)}, bf16[1,256,512]{2,1,0:T(8,128)(2,1)S(1)}, u32[]{:S(2)}, u32[]{:S(2)}) collective-permute-start(bf16[1,256,512]{2,1,0:T(8,128)(2,1)S(1)} %get-tuple-element.46), channel_id=1, source_target_pairs={{0,5},{1,4},{2,7},{3,6},{4,1},{5,0},{6,3},{7,2},{8,13},{9,12},{10,... | collective-permute-start | bytes 786440 | tf_op jit(solution)/shard_map/ppermute | solution.py:434
  141.4 33.2 %collective-permute-start.11 = (bf16[1,256,512]{2,1,0:T(8,128)(2,1)S(1)}, bf16[1,256,512]{2,1,0:T(8,128)(2,1)S(1)}, u32[]{:S(2)}, u32[]{:S(2)}) collective-permute-start(bf16[1,256,512]{2,1,0:T(8,128)(2,1)S(1)} %get-tuple-element.47), channel_id=1, source_target_pairs={{0,6},{1,7},{2,4},{3,5},{4,2},{5,3},{6,0},{7,1},{8,14},{9,15},{10,... | collective-permute-start | bytes 786440 | tf_op jit(solution)/shard_map/ppermute | solution.py:434
  143.4 31.2 %collective-permute-start.12 = (bf16[1,256,512]{2,1,0:T(8,128)(2,1)S(1)}, bf16[1,256,512]{2,1,0:T(8,128)(2,1)S(1)}, u32[]{:S(2)}, u32[]{:S(2)}) collective-permute-start(bf16[1,256,512]{2,1,0:T(8,128)(2,1)S(1)} %get-tuple-element.48), channel_id=1, source_target_pairs={{0,7},{1,6},{2,5},{3,4},{4,3},{5,2},{6,1},{7,0},{8,15},{9,14},{10,... | collective-permute-start | bytes 786440 | tf_op jit(solution)/shard_map/ppermute | solution.py:434
  154.6 28.5 %copy-start.16 = (f32[512,128]{1,0:T(8,128)}, f32[512,128]{1,0:T(8,128)S(1)}, u32[]{:S(2)}) copy-start(f32[512,128]{1,0:T(8,128)S(1)} %get-tuple-element.66) | copy-start | bytes 786436
  168.1 16.8 %collective-permute-start.31 = (f32[512,128]{1,0:T(8,128)}, f32[512,128]{1,0:T(8,128)}, u32[]{:S(2)}, u32[]{:S(2)}) collective-permute-start(f32[512,128]{1,0:T(8,128)} %get-tuple-element.67), channel_id=1, source_target_pairs={{0,8},{8,0},{16,24},{24,16},{1,9},{9,1},{17,25},{25,17},{2,10},{10... | collective-permute-start | bytes 786440 | tf_op jit(solution)/shard_map/ppermute | solution.py:434
  183.1 0.7 copy-start.17
  183.8 3.0 collective-permute-start.16
  186.0 14.6 %collective-permute-start.32 = (f32[512,128]{1,0:T(8,128)S(1)}, f32[512,128]{1,0:T(8,128)S(1)}, u32[]{:S(2)}, u32[]{:S(2)}) collective-permute-start(f32[512,128]{1,0:T(8,128)S(1)} %add.14), channel_id=1, source_target_pairs={{0,16},{8,24},{16,0},{24,8},{1,17},{9,25},{17,1},{25,9},{2,18},{10... | collective-permute-start | bytes 786440 | tf_op jit(solution)/shard_map/ppermute | solution.py:434
  187.8 12.5 %collective-permute-start.17 = (f32[512,128]{1,0:T(8,128)S(1)}, f32[512,128]{1,0:T(8,128)S(1)}, u32[]{:S(2)}, u32[]{:S(2)}) collective-permute-start(f32[512,128]{1,0:T(8,128)S(1)} %add.12), channel_id=1, source_target_pairs={{0,16},{8,24},{16,0},{24,8},{1,17},{9,25},{17,1},{25,9},{2,18},{10... | collective-permute-start | bytes 786440 | tf_op jit(solution)/shard_map/ppermute | solution.py:434
  189.2 12.7 %copy-start.8 = (bf16[2048,512]{1,0:T(8,128)(2,1)S(1)}, bf16[2048,512]{1,0:T(8,128)(2,1)}, u32[]{:S(2)}) copy-start(bf16[2048,512]{1,0:T(8,128)(2,1)} %copy-done.7) | copy-start | bytes 6291460
  200.5 1.4 collective-permute-start.19
  200.7 21.6 %copy-start.6 = (bf16[2048,512]{1,0:T(8,128)(2,1)S(1)}, bf16[2048,512]{1,0:T(8,128)(2,1)}, u32[]{:S(2)}) copy-start(bf16[2048,512]{1,0:T(8,128)(2,1)} %copy-done.5) | copy-start | bytes 6291460
  200.8 21.6 %collective-permute-start.33 = (bf16[512,128]{1,0:T(8,128)(2,1)S(1)}, bf16[512,128]{1,0:T(8,128)(2,1)S(1)}, u32[]{:S(2)}, u32[]{:S(2)}) collective-permute-start(bf16[512,128]{1,0:T(8,128)(2,1)S(1)} %fusion.1.refs_0_), channel_id=1, source_target_pairs={{0,8},{8,0},{16,24},{24,16},{1,9},{9,1},{17,25},{25,17},{2,10},{10... | collective-permute-start | bytes 393224 | tf_op jit(solution)/shard_map/ppermute | solution.py:434
  207.7 27.8 %collective-permute-start.20 = (bf16[256,512]{1,0:T(8,128)(2,1)S(1)}, bf16[256,512]{1,0:T(8,128)(2,1)S(1)}, u32[]{:S(2)}, u32[]{:S(2)}) collective-permute-start(bf16[256,512]{1,0:T(8,128)(2,1)S(1)} %get-tuple-element.52), channel_id=1, source_target_pairs={{0,7},{1,6},{2,5},{3,4},{4,3},{5,2},{6,1},{7,0},{8,15},{9,14},{10,... | collective-permute-start | bytes 786440 | tf_op jit(solution)/shard_map/ppermute | solution.py:434
  210.0 28.5 %collective-permute-start.21 = (bf16[256,512]{1,0:T(8,128)(2,1)S(1)}, bf16[256,512]{1,0:T(8,128)(2,1)S(1)}, u32[]{:S(2)}, u32[]{:S(2)}) collective-permute-start(bf16[256,512]{1,0:T(8,128)(2,1)S(1)} %get-tuple-element.53), channel_id=1, source_target_pairs={{0,6},{1,7},{2,4},{3,5},{4,2},{5,3},{6,0},{7,1},{8,14},{9,15},{10,... | collective-permute-start | bytes 786440 | tf_op jit(solution)/shard_map/ppermute | solution.py:434
  211.5 52.4 %collective-permute-start.22 = (bf16[256,512]{1,0:T(8,128)(2,1)S(1)}, bf16[256,512]{1,0:T(8,128)(2,1)S(1)}, u32[]{:S(2)}, u32[]{:S(2)}) collective-permute-start(bf16[256,512]{1,0:T(8,128)(2,1)S(1)} %get-tuple-element.54), channel_id=1, source_target_pairs={{0,5},{1,4},{2,7},{3,6},{4,1},{5,0},{6,3},{7,2},{8,13},{9,12},{10,... | collective-permute-start | bytes 786440 | tf_op jit(solution)/shard_map/ppermute | solution.py:434
  222.3 46.3 %collective-permute-start.23 = (bf16[256,512]{1,0:T(8,128)(2,1)S(1)}, bf16[256,512]{1,0:T(8,128)(2,1)S(1)}, u32[]{:S(2)}, u32[]{:S(2)}) collective-permute-start(bf16[256,512]{1,0:T(8,128)(2,1)S(1)} %get-tuple-element.55), channel_id=1, source_target_pairs={{0,4},{1,5},{2,6},{3,7},{4,0},{5,1},{6,2},{7,3},{8,12},{9,13},{10,... | collective-permute-start | bytes 786440 | tf_op jit(solution)/shard_map/ppermute | solution.py:434
  228.3 47.1 %collective-permute-start.34 = (bf16[256,512]{1,0:T(8,128)(2,1)S(1)}, bf16[256,512]{1,0:T(8,128)(2,1)S(1)}, u32[]{:S(2)}, u32[]{:S(2)}) collective-permute-start(bf16[256,512]{1,0:T(8,128)(2,1)S(1)} %get-tuple-element.68), channel_id=1, source_target_pairs={{0,7},{1,6},{2,5},{3,4},{4,3},{5,2},{6,1},{7,0},{8,15},{9,14},{10,... | collective-permute-start | bytes 786440 | tf_op jit(solution)/shard_map/ppermute | solution.py:434
  235.5 41.0 %collective-permute-start.35 = (bf16[256,512]{1,0:T(8,128)(2,1)S(1)}, bf16[256,512]{1,0:T(8,128)(2,1)S(1)}, u32[]{:S(2)}, u32[]{:S(2)}) collective-permute-start(bf16[256,512]{1,0:T(8,128)(2,1)S(1)} %get-tuple-element.69), channel_id=1, source_target_pairs={{0,6},{1,7},{2,4},{3,5},{4,2},{5,3},{6,0},{7,1},{8,14},{9,15},{10,... | collective-permute-start | bytes 786440 | tf_op jit(solution)/shard_map/ppermute | solution.py:434
  238.5 48.4 %collective-permute-start.24 = (bf16[256,512]{1,0:T(8,128)(2,1)S(1)}, bf16[256,512]{1,0:T(8,128)(2,1)S(1)}, u32[]{:S(2)}, u32[]{:S(2)}) collective-permute-start(bf16[256,512]{1,0:T(8,128)(2,1)S(1)} %get-tuple-element.57), channel_id=1, source_target_pairs={{0,3},{1,2},{2,1},{3,0},{4,7},{5,6},{6,5},{7,4},{8,11},{9,10},{10,... | collective-permute-start | bytes 786440 | tf_op jit(solution)/shard_map/ppermute | solution.py:434
  263.9 23.0 %collective-permute-start.25 = (bf16[256,512]{1,0:T(8,128)(2,1)S(1)}, bf16[256,512]{1,0:T(8,128)(2,1)S(1)}, u32[]{:S(2)}, u32[]{:S(2)}) collective-permute-start(bf16[256,512]{1,0:T(8,128)(2,1)S(1)} %get-tuple-element.58), channel_id=1, source_target_pairs={{0,2},{1,3},{2,0},{3,1},{4,6},{5,7},{6,4},{7,5},{8,10},{9,11},{10,... | collective-permute-start | bytes 786440 | tf_op jit(solution)/shard_map/ppermute | solution.py:434
  268.5 20.3 %collective-permute-start.26 = (bf16[256,512]{1,0:T(8,128)(2,1)S(1)}, bf16[256,512]{1,0:T(8,128)(2,1)S(1)}, u32[]{:S(2)}, u32[]{:S(2)}) collective-permute-start(bf16[256,512]{1,0:T(8,128)(2,1)S(1)} %get-tuple-element.59), channel_id=1, source_target_pairs={{0,1},{1,0},{2,3},{3,2},{4,5},{5,4},{6,7},{7,6},{8,9},{9,8},{10,11... | collective-permute-start | bytes 786440 | tf_op jit(solution)/shard_map/ppermute | solution.py:434
  270.0 20.3 %copy-start.1 = (bf16[8,256,1024]{2,1,0:T(8,128)(2,1)S(1)}, bf16[8,256,1024]{2,1,0:T(8,128)(2,1)}, u32[]{:S(2)}) copy-start(bf16[8,256,1024]{2,1,0:T(8,128)(2,1)} %copy-done) | copy-start | bytes 12582916
  270.0 20.3 %copy-start.11 = (bf16[128,1024]{1,0:T(8,128)(2,1)S(1)}, bf16[128,1024]{1,0:T(8,128)(2,1)}, u32[]{:S(2)}) copy-start(bf16[128,1024]{1,0:T(8,128)(2,1)} %copy-done.9) | copy-start | bytes 786436
  270.0 20.3 %copy-start.13 = (bf16[128,1024]{1,0:T(8,128)(2,1)S(1)}, bf16[128,1024]{1,0:T(8,128)(2,1)}, u32[]{:S(2)}) copy-start(bf16[128,1024]{1,0:T(8,128)(2,1)} %copy-done.12) | copy-start | bytes 786436
  270.0 20.3 %copy-start.15 = (bf16[128,1024]{1,0:T(8,128)(2,1)S(1)}, bf16[128,1024]{1,0:T(8,128)(2,1)}, u32[]{:S(2)}) copy-start(bf16[128,1024]{1,0:T(8,128)(2,1)} %copy-done.14) | copy-start | bytes 786436
  275.5 22.2 %collective-permute-start.36 = (bf16[256,512]{1,0:T(8,128)(2,1)S(1)}, bf16[256,512]{1,0:T(8,128)(2,1)S(1)}, u32[]{:S(2)}, u32[]{:S(2)}) collective-permute-start(bf16[256,512]{1,0:T(8,128)(2,1)S(1)} %get-tuple-element.70), channel_id=1, source_target_pairs={{0,5},{1,4},{2,7},{3,6},{4,1},{5,0},{6,3},{7,2},{8,13},{9,12},{10,... | collective-permute-start | bytes 786440 | tf_op jit(solution)/shard_map/ppermute | solution.py:434
  276.5 25.8 %collective-permute-start.37 = (bf16[256,512]{1,0:T(8,128)(2,1)S(1)}, bf16[256,512]{1,0:T(8,128)(2,1)S(1)}, u32[]{:S(2)}, u32[]{:S(2)}) collective-permute-start(bf16[256,512]{1,0:T(8,128)(2,1)S(1)} %get-tuple-element.71), channel_id=1, source_target_pairs={{0,4},{1,5},{2,6},{3,7},{4,0},{5,1},{6,2},{7,3},{8,12},{9,13},{10,... | collective-permute-start | bytes 786440 | tf_op jit(solution)/shard_map/ppermute | solution.py:434
  286.9 17.7 %collective-permute-start.38 = (bf16[256,512]{1,0:T(8,128)(2,1)S(1)}, bf16[256,512]{1,0:T(8,128)(2,1)S(1)}, u32[]{:S(2)}, u32[]{:S(2)}) collective-permute-start(bf16[256,512]{1,0:T(8,128)(2,1)S(1)} %get-tuple-element.73), channel_id=1, source_target_pairs={{0,3},{1,2},{2,1},{3,0},{4,7},{5,6},{6,5},{7,4},{8,11},{9,10},{10,... | collective-permute-start | bytes 786440 | tf_op jit(solution)/shard_map/ppermute | solution.py:434
  286.9 21.1 %collective-permute-start.39 = (bf16[256,512]{1,0:T(8,128)(2,1)S(1)}, bf16[256,512]{1,0:T(8,128)(2,1)S(1)}, u32[]{:S(2)}, u32[]{:S(2)}) collective-permute-start(bf16[256,512]{1,0:T(8,128)(2,1)S(1)} %get-tuple-element.74), channel_id=1, source_target_pairs={{0,2},{1,3},{2,0},{3,1},{4,6},{5,7},{6,4},{7,5},{8,10},{9,11},{10,... | collective-permute-start | bytes 786440 | tf_op jit(solution)/shard_map/ppermute | solution.py:434
  288.9 19.1 %collective-permute-start.40 = (bf16[256,512]{1,0:T(8,128)(2,1)S(1)}, bf16[256,512]{1,0:T(8,128)(2,1)S(1)}, u32[]{:S(2)}, u32[]{:S(2)}) collective-permute-start(bf16[256,512]{1,0:T(8,128)(2,1)S(1)} %get-tuple-element.75), channel_id=1, source_target_pairs={{0,1},{1,0},{2,3},{3,2},{4,5},{5,4},{6,7},{7,6},{8,9},{9,8},{10,11... | collective-permute-start | bytes 786440 | tf_op jit(solution)/shard_map/ppermute | solution.py:434
